TPU v7x, 32 devices: a whole 2x2x4 slice. The times are simulated.
32 devices in a mesh: dp: 8 (over z, x), mp: 4 (over y, core).
Axes of the slice: x: 2, y: 2, z: 4, core: 2. Of those that a mesh axis runs over, the one named last changes fastest.
Arguments:
- interface: float32 [8192, 512], P(('dp', 'mp')), may hold values from -6 to 6
- latents: float32 [1024, 1024], P(('dp', 'mp')), may hold values from -6 to 6
- keep_mask: int32 [8, 1024], P('dp'), may hold values from 0 to 1, as said below
- read_gain_lat: float32 [1024], replicated, may hold values from 0.25 to 1.75
- read_gain_int: float32 [512], replicated, may hold values from 0.25 to 1.75
- read_query: float32 [1024, 1024], P(None, 'mp'), may hold values from -0.1875 to 0.1875
- read_keyval: float32 [2, 512, 1024], P(None, None, 'mp'), may hold values from -0.25 to 0.25
- read_out: float32 [1024, 1024], P('mp'), may hold values from -3 to 3
- read_gain_mlp: float32 [1024], replicated, may hold values from 0.25 to 1.75
- read_up: float32 [1024, 4096], P(None, 'mp'), may hold values from -0.1875 to 0.1875
- read_down: float32 [4096, 1024], P('mp'), may hold values from -0.09375 to 0.09375
- self_gain_att: float32 [2, 1024], replicated, may hold values from 0.25 to 1.75
- self_qkv: float32 [2, 3, 1024, 1024], P(None, None, None, 'mp'), may hold values from -0.1875 to 0.1875
- self_out: float32 [2, 1024, 1024], P(None, 'mp'), may hold values from -1.5 to 1.5
- self_gain_mlp: float32 [2, 1024], replicated, may hold values from 0.25 to 1.75
- self_up: float32 [2, 1024, 4096], P(None, None, 'mp'), may hold values from -0.1875 to 0.1875
- self_down: float32 [2, 4096, 1024], P(None, 'mp'), may hold values from -0.09375 to 0.09375
- write_gain_int: float32 [512], replicated, may hold values from 0.25 to 1.75
- write_gain_lat: float32 [1024], replicated, may hold values from 0.25 to 1.75
- write_query: float32 [512, 512], P(None, 'mp'), may hold values from -0.25 to 0.25
- write_keyval: float32 [2, 1024, 512], P(None, None, 'mp'), may hold values from -0.1875 to 0.1875
- write_out: float32 [512, 512], P('mp'), may hold values from -1.5 to 1.5
- write_gain_mlp: float32 [512], replicated, may hold values from 0.25 to 1.75
- write_up: float32 [512, 2048], P(None, 'mp'), may hold values from -0.25 to 0.25
- write_down: float32 [2048, 512], P('mp'), may hold values from -0.125 to 0.125
- grad_interface_out: float32 [8192, 512], P(('dp', 'mp')), may hold values from -6 to 6
- grad_latents_out: float32 [1024, 1024], P(('dp', 'mp')), may hold values from -6 to 6
Outputs:
- interface_out: float32 [8192, 512], P(('dp', 'mp'))
- latents_out: float32 [1024, 1024], P(('dp', 'mp'))
- grad_interface: float32 [8192, 512], P(('dp', 'mp'))
- grad_latents: float32 [1024, 1024], P(('dp', 'mp'))
- grad_read_gain_lat: float32 [1024], replicated
- grad_read_gain_int: float32 [512], replicated
- grad_read_query: float32 [1024, 1024], P(None, 'mp')
- grad_read_keyval: float32 [2, 512, 1024], P(None, None, 'mp')
- grad_read_out: float32 [1024, 1024], P('mp')
- grad_read_gain_mlp: float32 [1024], replicated
- grad_read_up: float32 [1024, 4096], P(None, 'mp')
- grad_read_down: float32 [4096, 1024], P('mp')
- grad_self_gain_att: float32 [2, 1024], replicated
- grad_self_qkv: float32 [2, 3, 1024, 1024], P(None, None, None, 'mp')
- grad_self_out: float32 [2, 1024, 1024], P(None, 'mp')
- grad_self_gain_mlp: float32 [2, 1024], replicated
- grad_self_up: float32 [2, 1024, 4096], P(None, None, 'mp')
- grad_self_down: float32 [2, 4096, 1024], P(None, 'mp')
- grad_write_gain_int: float32 [512], replicated
- grad_write_gain_lat: float32 [1024], replicated
- grad_write_query: float32 [512, 512], P(None, 'mp')
- grad_write_keyval: float32 [2, 1024, 512], P(None, None, 'mp')
- grad_write_out: float32 [512, 512], P('mp')
- grad_write_gain_mlp: float32 [512], replicated
- grad_write_up: float32 [512, 2048], P(None, 'mp')
- grad_write_down: float32 [2048, 512], P('mp')
Inputs may be any that keep to these rules, and one draw needn't show every extreme that they name: `keep_mask`: each image keeps one patch or more.
All inputs are finite; a program needn't handle non-finite values.
Results may differ from a plain program's by a relative error of at most 0.0003.
Values sent between devices are 32-bit elements; how exact they have to be, the bound alone decides.
No kernel may reach another device: no remote copies, remote signals or barrier semaphores. Data moves between devices by JAX's collectives and lax.ppermute only.
A program may use at most 256 MiB of HBM per device.

v0:
```python
import math
import jax
import jax.numpy as jnp
from jax import lax
from jax.sharding import PartitionSpec as P

D = 1024
E = 512
HEADS = 16
LATENTS = 128
LAYERS = 2
EPSILON = 1e-05
PRECISE = lax.Precision.HIGHEST
MASK_FILL = -1000000000.0


def layer_norm(values, gain_vec):
    centre = jnp.mean(values, axis=-1, keepdims=True)
    centred = values - centre
    spread = jnp.mean(centred * centred, axis=-1, keepdims=True)
    return centred * lax.rsqrt(spread + EPSILON) * gain_vec


def product(left_side, right_side):
    return jnp.dot(left_side, right_side, precision=PRECISE)


def contract_rows(left_side, right_side):
    return lax.dot_general(left_side, right_side, (((0,), (0,)), ((), ())), precision=PRECISE)


def contract_last(left_side, right_side):
    return lax.dot_general(left_side, right_side, (((1,), (1,)), ((), ())), precision=PRECISE)


def attention(queries, keys_in, values_in, key_bias, images, head_width):
    query_len = queries.shape[0] // images
    key_len = keys_in.shape[0] // images
    head_count = queries.shape[1] // head_width
    query_heads = queries.reshape(images, query_len, head_count, head_width)
    key_heads = keys_in.reshape(images, key_len, head_count, head_width)
    value_heads = values_in.reshape(images, key_len, head_count, head_width)
    scores = jnp.einsum("bqhd,bkhd->bhqk", query_heads, key_heads, precision=PRECISE)
    scores = scores / math.sqrt(head_width) + key_bias[:, None, None, :]
    weights = jax.nn.softmax(scores, axis=-1)
    mixture = jnp.einsum("bhqk,bkhd->bqhd", weights, value_heads, precision=PRECISE)
    return mixture.reshape(images * query_len, head_count * head_width)


def attend_local(query_norm, key_norm, w_query, w_key, w_value, key_bias, head_width):
    return attention(
        product(query_norm, w_query),
        product(key_norm, w_key),
        product(key_norm, w_value),
        key_bias,
        key_bias.shape[0],
        head_width,
    )


def expand(norm_full, w_up):
    return jax.nn.gelu(product(norm_full, w_up))


def gather_rows(pieces_in):
    return lax.all_gather(pieces_in, "mp", axis=0, tiled=True)


def branch_sum(source, weight):
    return lax.psum_scatter(product(source, weight), "mp", scatter_dimension=0, tiled=True)


def spread_grad(grad_shard):
    return lax.all_gather(grad_shard, "mp", axis=0, tiled=True)


def collect_grads(pieces_in):
    return lax.psum_scatter(pieces_in, "mp", scatter_dimension=0, tiled=True)


def reduce_branch(weight_grads):
    return lax.psum(weight_grads, "dp")


def norm_backward(source, gain_vec, grad_normed):
    normed, pull_back = jax.vjp(layer_norm, source, gain_vec)
    return pull_back(grad_normed)


def norms_of(query_src, key_src, query_gain, key_gain, crossed):
    if crossed:
        gathered = gather_rows((layer_norm(query_src, query_gain), layer_norm(key_src, key_gain)))
        return (gathered[0], gathered[1])
    gathered = gather_rows((layer_norm(query_src, query_gain),))
    return (gathered[0], gathered[0])


def attend_forward(
    query_src,
    key_src,
    query_gain,
    key_gain,
    w_query,
    w_key,
    w_value,
    w_out,
    key_bias,
    head_width,
    crossed,
):
    query_norm, key_norm = norms_of(query_src, key_src, query_gain, key_gain, crossed)
    mixture = attend_local(query_norm, key_norm, w_query, w_key, w_value, key_bias, head_width)
    return (query_src + branch_sum(mixture, w_out), (query_norm, key_norm))


def attend_backward(
    grad_shard,
    query_src,
    key_src,
    query_gain,
    key_gain,
    w_query,
    w_key,
    w_value,
    w_out,
    key_bias,
    head_width,
    crossed,
):
    query_norm, key_norm = norms_of(query_src, key_src, query_gain, key_gain, crossed)
    if crossed:
        mixture, pull_back = jax.vjp(
            lambda query_in, key_in, query_weight, key_weight, value_weight: attend_local(
                query_in, key_in, query_weight, key_weight, value_weight, key_bias, head_width
            ),
            query_norm,
            key_norm,
            w_query,
            w_key,
            w_value,
        )
    else:
        mixture, pull_back = jax.vjp(
            lambda query_in, query_weight, key_weight, value_weight: attend_local(
                query_in, query_in, query_weight, key_weight, value_weight, key_bias, head_width
            ),
            query_norm,
            w_query,
            w_key,
            w_value,
        )
    grad_full = spread_grad(grad_shard)
    grad_out_weight = contract_rows(mixture, grad_full)
    pulled = pull_back(contract_last(grad_full, w_out))
    if crossed:
        query_part, key_part = collect_grads((pulled[0], pulled[1]))
        grad_query_src, gain_query = norm_backward(query_src, query_gain, query_part)
        grad_key_src, gain_key = norm_backward(key_src, key_gain, key_part)
        weight_grads = reduce_branch((pulled[2], pulled[3], pulled[4], grad_out_weight))
        return (grad_query_src, grad_key_src, (gain_query, gain_key), weight_grads)
    collected = collect_grads((pulled[0],))
    grad_query_src, gain_query = norm_backward(query_src, query_gain, collected[0])
    weight_grads = reduce_branch((pulled[1], pulled[2], pulled[3], grad_out_weight))
    return (grad_query_src, None, (gain_query,), weight_grads)


def expand_forward(stream, gain_vec, w_up, w_down):
    gathered = gather_rows((layer_norm(stream, gain_vec),))
    norm_full = gathered[0]
    return (stream + branch_sum(expand(norm_full, w_up), w_down), norm_full)


def expand_backward(grad_shard, stream, gain_vec, w_up, w_down):
    norm_full = gather_rows((layer_norm(stream, gain_vec),))[0]
    hidden, pull_back = jax.vjp(expand, norm_full, w_up)
    grad_full = spread_grad(grad_shard)
    grad_down = contract_rows(hidden, grad_full)
    grad_norm_full, grad_up = pull_back(contract_last(grad_full, w_down))
    collected = collect_grads((grad_norm_full,))
    grad_stream, grad_gain = norm_backward(stream, gain_vec, collected[0])
    return (grad_shard + grad_stream, grad_gain, reduce_branch((grad_up, grad_down)))


def body(
    interface,
    latents,
    keep_mask,
    read_gain_lat,
    read_gain_int,
    read_query,
    read_keyval,
    read_out,
    read_gain_mlp,
    read_up,
    read_down,
    self_gain_att,
    self_qkv,
    self_out,
    self_gain_mlp,
    self_up,
    self_down,
    write_gain_int,
    write_gain_lat,
    write_query,
    write_keyval,
    write_out,
    write_gain_mlp,
    write_up,
    write_down,
    grad_interface_out,
    grad_latents_out,
):
    images = keep_mask.shape[0]
    shard_rows = interface.shape[0]
    flat_keep = keep_mask.reshape(-1).astype(jnp.float32)
    keep_rows = lax.dynamic_slice_in_dim(
        flat_keep, lax.axis_index("mp") * shard_rows, shard_rows, 0
    )[:, None]
    stream_x0 = interface * keep_rows
    read_bias = jnp.where(keep_mask > 0, 0.0, MASK_FILL).astype(jnp.float32)
    open_bias = jnp.zeros((images, LATENTS), jnp.float32)
    latent_head = D // HEADS
    patch_head = E // HEADS
    stream_z1, read_stored = attend_forward(
        latents,
        stream_x0,
        read_gain_lat,
        read_gain_int,
        read_query,
        read_keyval[0],
        read_keyval[1],
        read_out,
        read_bias,
        latent_head,
        True,
    )
    stream_z, read_mlp_stored = expand_forward(stream_z1, read_gain_mlp, read_up, read_down)
    layer_store = []
    for layer_idx in range(LAYERS):
        attend_input = stream_z
        stream_mid, attend_stored = attend_forward(
            attend_input,
            attend_input,
            self_gain_att[layer_idx],
            self_gain_att[layer_idx],
            self_qkv[layer_idx, 0],
            self_qkv[layer_idx, 1],
            self_qkv[layer_idx, 2],
            self_out[layer_idx],
            open_bias,
            latent_head,
            False,
        )
        stream_z, expand_stored = expand_forward(
            stream_mid, self_gain_mlp[layer_idx], self_up[layer_idx], self_down[layer_idx]
        )
        layer_store.append((attend_input, attend_stored, stream_mid, expand_stored))
    stream_x1, write_stored = attend_forward(
        stream_x0,
        stream_z,
        write_gain_int,
        write_gain_lat,
        write_query,
        write_keyval[0],
        write_keyval[1],
        write_out,
        open_bias,
        patch_head,
        True,
    )
    interface_out, write_mlp_stored = expand_forward(
        stream_x1, write_gain_mlp, write_up, write_down
    )
    grad_x, gain_write_mlp, grads_write_mlp = expand_backward(
        grad_interface_out, stream_x1, write_gain_mlp, write_up, write_down
    )
    grad_query, grad_key, gains_write, grads_write = attend_backward(
        grad_x,
        stream_x0,
        stream_z,
        write_gain_int,
        write_gain_lat,
        write_query,
        write_keyval[0],
        write_keyval[1],
        write_out,
        open_bias,
        patch_head,
        True,
    )
    grad_x = grad_x + grad_query
    grad_z = grad_latents_out + grad_key
    gains_att_list = [None] * LAYERS
    gains_mlp_list = [None] * LAYERS
    grads_att_list = [None] * LAYERS
    grads_mlp_list = [None] * LAYERS
    for layer_idx in reversed(range(LAYERS)):
        attend_input, attend_stored, stream_mid, expand_stored = layer_store[layer_idx]
        grad_z, gain_mlp_layer, grads_mlp_layer = expand_backward(
            grad_z, stream_mid, self_gain_mlp[layer_idx], self_up[layer_idx], self_down[layer_idx]
        )
        grad_self, unused, gains_att_layer, grads_att_layer = attend_backward(
            grad_z,
            attend_input,
            attend_input,
            self_gain_att[layer_idx],
            self_gain_att[layer_idx],
            self_qkv[layer_idx, 0],
            self_qkv[layer_idx, 1],
            self_qkv[layer_idx, 2],
            self_out[layer_idx],
            open_bias,
            latent_head,
            False,
        )
        grad_z = grad_z + grad_self
        gains_att_list[layer_idx] = gains_att_layer[0]
        gains_mlp_list[layer_idx] = gain_mlp_layer
        grads_att_list[layer_idx] = grads_att_layer
        grads_mlp_list[layer_idx] = grads_mlp_layer
    grad_z, gain_read_mlp, grads_read_mlp = expand_backward(
        grad_z, stream_z1, read_gain_mlp, read_up, read_down
    )
    grad_query, grad_key, gains_read, grads_read = attend_backward(
        grad_z,
        latents,
        stream_x0,
        read_gain_lat,
        read_gain_int,
        read_query,
        read_keyval[0],
        read_keyval[1],
        read_out,
        read_bias,
        latent_head,
        True,
    )
    grad_z = grad_z + grad_query
    grad_x = grad_x + grad_key
    grad_interface = grad_x * keep_rows
    summed_gains = lax.psum(
        (
            gains_read[0],
            gains_read[1],
            gain_read_mlp,
            jnp.stack(gains_att_list),
            jnp.stack(gains_mlp_list),
            gains_write[0],
            gains_write[1],
            gain_write_mlp,
        ),
        ("dp", "mp"),
    )
    self_qkv_grad = jnp.stack(
        [jnp.stack([entry[0], entry[1], entry[2]]) for entry in grads_att_list]
    )
    self_out_grad = jnp.stack([entry[3] for entry in grads_att_list])
    self_up_grad = jnp.stack([entry[0] for entry in grads_mlp_list])
    self_down_grad = jnp.stack([entry[1] for entry in grads_mlp_list])
    weight_tuple = (
        grads_read[0],
        jnp.stack([grads_read[1], grads_read[2]]),
        grads_read[3],
        grads_read_mlp[0],
        grads_read_mlp[1],
        self_qkv_grad,
        self_out_grad,
        self_up_grad,
        self_down_grad,
        grads_write[0],
        jnp.stack([grads_write[1], grads_write[2]]),
        grads_write[3],
        grads_write_mlp[0],
        grads_write_mlp[1],
    )
    return (
        interface_out,
        stream_z,
        grad_interface,
        grad_z,
        summed_gains[0],
        summed_gains[1],
        weight_tuple[0],
        weight_tuple[1],
        weight_tuple[2],
        summed_gains[2],
        weight_tuple[3],
        weight_tuple[4],
        summed_gains[3],
        weight_tuple[5],
        weight_tuple[6],
        summed_gains[4],
        weight_tuple[7],
        weight_tuple[8],
        summed_gains[5],
        summed_gains[6],
        weight_tuple[9],
        weight_tuple[10],
        weight_tuple[11],
        summed_gains[7],
        weight_tuple[12],
        weight_tuple[13],
    )


def solution(mesh):
    in_specs = (
        P(("dp", "mp"), None),
        P(("dp", "mp"), None),
        P("dp", None),
        P(),
        P(),
        P(None, "mp"),
        P(None, None, "mp"),
        P("mp", None),
        P(),
        P(None, "mp"),
        P("mp", None),
        P(),
        P(None, None, None, "mp"),
        P(None, "mp", None),
        P(),
        P(None, None, "mp"),
        P(None, "mp", None),
        P(),
        P(),
        P(None, "mp"),
        P(None, None, "mp"),
        P("mp", None),
        P(),
        P(None, "mp"),
        P("mp", None),
        P(("dp", "mp"), None),
        P(("dp", "mp"), None),
    )
    out_specs = (
        P(("dp", "mp"), None),
        P(("dp", "mp"), None),
        P(("dp", "mp"), None),
        P(("dp", "mp"), None),
        P(),
        P(),
        P(None, "mp"),
        P(None, None, "mp"),
        P("mp", None),
        P(),
        P(None, "mp"),
        P("mp", None),
        P(),
        P(None, None, None, "mp"),
        P(None, "mp", None),
        P(),
        P(None, None, "mp"),
        P(None, "mp", None),
        P(),
        P(),
        P(None, "mp"),
        P(None, None, "mp"),
        P("mp", None),
        P(),
        P(None, "mp"),
        P("mp", None),
    )
    return jax.shard_map(body, mesh=mesh, in_specs=in_specs, out_specs=out_specs, check_vma=False)
```

profile of v0, /device:TPU:0, one launch (start us, length us, event | category | flops | bytes accessed | tf_op | source)
XLA Modules:
  0.0 2203.9 jit_solution(14452684715133826007)
XLA Ops:
  19.0 10.0 all_gather.65
  30.8 8.7 all-gather.6.cloned.1.call-done
  53.9 22.6 %reduce-scatter.19.cloned.1.call-done = f32[32,1024]{1,0:T(8,128)} async-done(((f32[128,1024]{1,0:T(8,128)}), f32[32,1024]{1,0:T(8,128)}) %reduce-scatter.19.cloned.1.call-update) | async-done | bytes 131088 | tf_op jit(solution)/shard_map/reduce_scatter | solution.py:70
  78.8 7.1 all_gather.66
  95.0 5.5 slice_bitcast_fusion
  108.2 8.9 reduce-scatter.21.cloned.1.call-done
  119.2 6.9 all_gather.67
  134.0 21.3 reduce-scatter.23.cloned.1.call-done
  157.2 7.0 all_gather.68
  169.8 5.5 fusion.10
  183.0 14.5 reduce-scatter.25.cloned.1.call-done
  199.6 6.9 all_gather.69
  214.3 21.4 reduce-scatter.27.cloned.1.call-done
  237.6 7.2 all_gather.70
  250.7 5.5 fusion.2
  267.3 18.1 reduce-scatter.29.cloned.1.call-done
  287.4 6.8 all_gather.71
  305.2 31.3 %reduce-scatter.31.cloned.1.call-done = f32[256,512]{1,0:T(8,128)} async-done(((f32[1024,512]{1,0:T(8,128)}), f32[256,512]{1,0:T(8,128)}) %reduce-scatter.31.cloned.1.call-update) | async-done | bytes 524304 | tf_op jit(solution)/shard_map/reduce_scatter | solution.py:70
  340.5 20.1 all-gather.12.cloned.1.call-done
  360.6 6.6 fusion.207
  367.2 18.2 all-gather.10.cloned.1.call-done
  385.5 9.6 fusion.29
  402.4 6.9 fusion.54
  409.4 23.4 %reduce-scatter.35.cloned.1.call-done = f32[256,512]{1,0:T(8,128)} async-done(((f32[1024,512]{1,0:T(8,128)}), f32[256,512]{1,0:T(8,128)}) %reduce-scatter.35.cloned.1.call-update) | async-done | bytes 524304 | tf_op jit(solution)/shard_map/reduce_scatter | solution.py:78
  435.9 31.4 %reduce-scatter.33.cloned.1.call-done = f32[256,512]{1,0:T(8,128)} async-done(((f32[1024,512]{1,0:T(8,128)}), f32[256,512]{1,0:T(8,128)}) %reduce-scatter.33.cloned.1.call-update) | async-done | bytes 524304 | tf_op jit(solution)/shard_map/reduce_scatter | solution.py:70
  470.5 22.7 %all-gather.14.cloned.1.call-done = f32[1024,512]{1,0:T(8,128)} async-done(((f32[256,512]{1,0:T(8,128)}), f32[1024,512]{1,0:T(8,128)}) %all-gather.14.cloned.1.call-update) | async-done | bytes 2097168 | tf_op jit(solution)/shard_map/all_gather | solution.py:74
  508.6 21.8 reduce-scatter.39.cloned.1.call-done
  533.9 7.2 all_gather.76
  541.0 6.9 fusion.75
  548.7 7.3 fusion.4
  559.4 18.9 reduce-scatter.41.cloned.1.call-done
  581.2 7.1 all_gather.77
  600.2 22.1 %reduce-scatter.43.cloned.1.call-done = f32[32,1024]{1,0:T(8,128)} async-done(((f32[128,1024]{1,0:T(8,128)}), f32[32,1024]{1,0:T(8,128)}) %reduce-scatter.43.cloned.1.call-update) | async-done | bytes 131088 | tf_op jit(solution)/shard_map/reduce_scatter | solution.py:78
  625.9 7.0 all_gather.78
  632.9 6.9 fusion.69
  640.6 7.4 fusion.12
  648.1 22.1 %reduce-scatter.45.cloned.1.call-done = f32[32,1024]{1,0:T(8,128)} async-done(((f32[128,1024]{1,0:T(8,128)}), f32[32,1024]{1,0:T(8,128)}) %reduce-scatter.45.cloned.1.call-update) | async-done | bytes 131088 | tf_op jit(solution)/shard_map/reduce_scatter | solution.py:78
  673.2 7.2 all_gather.79
  692.2 22.2 %reduce-scatter.47.cloned.1.call-done = f32[32,1024]{1,0:T(8,128)} async-done(((f32[128,1024]{1,0:T(8,128)}), f32[32,1024]{1,0:T(8,128)}) %reduce-scatter.47.cloned.1.call-update) | async-done | bytes 131088 | tf_op jit(solution)/shard_map/reduce_scatter | solution.py:78
  717.2 7.2 all_gather.80
  724.4 6.8 fusion.213
  738.1 21.5 reduce-scatter.49.cloned.1.call-done
  763.3 7.0 all_gather.81
  789.2 6.9 fusion.222
  868.4 5.5 fusion.178
  893.9 47.7 %all-reduce = (f32[1024]{0:T(1024)}, f32[512]{0:T(512)}, f32[1024]{0:T(1024)}, f32[2,1024]{1,0:T(2,128)}, f32[2,1024]{1,0:T(2,128)}, /*index=5*/f32[512]{0:T(512)}, f32[1024]{0:T(1024)}, f32[512]{0:T(512)}) all-reduce(f32[1024]{0:T(1024)S(1)} %get-tuple-element.48, ...), channel_id=1, replica_groups=mesh['dp'=8,'mp'=4] {'dp','mp'}, use_global_device_ids=true, to_apply=%region_69.70 | all-reduce | flops 8704 | bytes 69632 | tf_op jit(solution)/shard_map/psum | solution.py:341
  942.8 1218.9 %all-reduce.4.cloned.1.call-done = (f32[1024,256]{1,0:T(8,128)}, f32[1,512,256]{2,1,0:T(8,128)}, f32[1,512,256]{2,1,0:T(8,128)}, f32[256,1024]{1,0:T(8,128)}, f3...) async-done(((f32[1024,256]{1,0:T(8,128)}, ...) | async-done | bytes 40370192 | tf_op jit(solution)/shard_map/psum | solution.py:82
  2177.7 6.8 pad_maximum_fusion
  (814 shorter events, 339.5 us)
Async XLA Ops:
  7.2 378.3 %copy-start = (f32[512,512]{1,0:T(8,128)S(1)}, f32[512,512]{1,0:T(8,128)}, u32[]{:S(2)}) copy-start(f32[512,512]{1,0:T(8,128)} %param.50) | copy-start | bytes 3145732
  7.2 32.3 %all-gather.6.cloned.1.call-start = ((), (), s32[]{:S(2)}) async-start(), calls=%async_computation.18 | async-start | bytes 2621440 | tf_op jit(solution)/shard_map/all_gather | solution.py:66
  12.9 63.6 %reduce-scatter.19.cloned.1.call-start = ((), (), s32[]{:S(2)}) async-start(), calls=%async_computation.19 | async-start | bytes 655360 | tf_op jit(solution)/shard_map/reduce_scatter | solution.py:70
  53.8 63.3 %reduce-scatter.21.cloned.1.call-start = ((), (), s32[]{:S(2)}) async-start(), calls=%async_computation.20 | async-start | bytes 655360 | tf_op jit(solution)/shard_map/reduce_scatter | solution.py:70
  95.0 60.3 %reduce-scatter.23.cloned.1.call-start = ((), (), s32[]{:S(2)}) async-start(), calls=%async_computation.21 | async-start | bytes 655360 | tf_op jit(solution)/shard_map/reduce_scatter | solution.py:70
  108.2 91.2 %copy-start.183 = (f32[1,1024]{1,0:T(1,128)}, f32[1,1024]{1,0:T(1,128)S(1)}, u32[]{:S(2)}) copy-start(f32[1,1024]{1,0:T(1,128)S(1)} %get-tuple-element.131) | copy-start | bytes 12292
  133.2 64.3 %reduce-scatter.25.cloned.1.call-start = ((), (), s32[]{:S(2)}) async-start(), calls=%async_computation.22 | async-start | bytes 655360 | tf_op jit(solution)/shard_map/reduce_scatter | solution.py:70
  134.0 35.0 %copy-start.185 = (f32[1,1024]{1,0:T(1,128)}, f32[1,1024]{1,0:T(1,128)S(1)}, u32[]{:S(2)}) copy-start(f32[1,1024]{1,0:T(1,128)S(1)} %get-tuple-element.130) | copy-start | bytes 12292
  134.0 103.5 %copy-start.187 = (f32[1,1024]{1,0:T(1,128)}, f32[1,1024]{1,0:T(1,128)S(1)}, u32[]{:S(2)}) copy-start(f32[1,1024]{1,0:T(1,128)S(1)} %get-tuple-element.129) | copy-start | bytes 12292
  175.3 60.3 %reduce-scatter.27.cloned.1.call-start = ((), (), s32[]{:S(2)}) async-start(), calls=%async_computation.23 | async-start | bytes 655360 | tf_op jit(solution)/shard_map/reduce_scatter | solution.py:70
  213.5 49.2 %all-gather.8.cloned.1.call-start = ((), (), s32[]{:S(2)}) async-start(), calls=%async_computation.25 | async-start | bytes 2621440 | tf_op jit(solution)/shard_map/all_gather | solution.py:66
  214.2 71.2 %reduce-scatter.29.cloned.1.call-start = ((), (), s32[]{:S(2)}) async-start(), calls=%async_computation.24 | async-start | bytes 655360 | tf_op jit(solution)/shard_map/reduce_scatter | solution.py:70
  256.3 80.2 %reduce-scatter.31.cloned.1.call-start = ((), (), s32[]{:S(2)}) async-start(), calls=%async_computation.26 | async-start | bytes 2621440 | tf_op jit(solution)/shard_map/reduce_scatter | solution.py:70
  304.6 56.0 %all-gather.12.cloned.1.call-start = ((), (), s32[]{:S(2)}) async-start(), calls=%async_computation.29 | async-start | bytes 2621440 | tf_op jit(solution)/shard_map/all_gather | solution.py:74
  305.2 80.3 %all-gather.10.cloned.1.call-start = ((), (), s32[]{:S(2)}) async-start(), calls=%async_computation.27 | async-start | bytes 2621440 | tf_op jit(solution)/shard_map/all_gather | solution.py:66
  340.3 92.5 %reduce-scatter.35.cloned.1.call-start = ((), (), s32[]{:S(2)}) async-start(), calls=%async_computation.30 | async-start | bytes 2621440 | tf_op jit(solution)/shard_map/reduce_scatter | solution.py:78
  401.2 66.1 %reduce-scatter.33.cloned.1.call-start = ((), (), s32[]{:S(2)}) async-start(), calls=%async_computation.28 | async-start | bytes 2621440 | tf_op jit(solution)/shard_map/reduce_scatter | solution.py:70
  409.3 60.2 %copy-start.111 = (f32[256,512]{1,0:T(8,128)S(1)}, f32[256,512]{1,0:T(8,128)}, u32[]{:S(2)}) copy-start(f32[256,512]{1,0:T(8,128)} %param.52) | copy-start | bytes 1572868
  409.3 83.9 %all-gather.14.cloned.1.call-start = ((), (), s32[]{:S(2)}) async-start(), calls=%async_computation.31 | async-start | bytes 2621440 | tf_op jit(solution)/shard_map/all_gather | solution.py:74
  470.5 59.9 %reduce-scatter.39.cloned.1.call-start = ((), (), s32[]{:S(2)}) async-start(), calls=%async_computation.33 | async-start | bytes 655360 | tf_op jit(solution)/shard_map/reduce_scatter | solution.py:78
  507.0 34.0 %copy-start.34 = (f32[128,1024]{1,0:T(8,128)S(1)}, f32[128,1024]{1,0:T(8,128)}, u32[]{:S(2)}) copy-start(f32[128,1024]{1,0:T(8,128)} %copy-done.33) | copy-start | bytes 1572868
  508.5 69.7 %reduce-scatter.41.cloned.1.call-start = ((), (), s32[]{:S(2)}) async-start(), calls=%async_computation.34 | async-start | bytes 655360 | tf_op jit(solution)/shard_map/reduce_scatter | solution.py:78
  556.1 66.2 %reduce-scatter.43.cloned.1.call-start = ((), (), s32[]{:S(2)}) async-start(), calls=%async_computation.35 | async-start | bytes 655360 | tf_op jit(solution)/shard_map/reduce_scatter | solution.py:78
  559.3 30.0 %copy-start.107 = (f32[4,128,128]{1,2,0:T(8,128)S(1)}, f32[4,128,128]{1,2,0:T(8,128)}, u32[]{:S(2)}) copy-start(f32[4,128,128]{1,2,0:T(8,128)} %copy-done.106) | copy-start | bytes 786436
  559.3 30.0 %copy-start.207 = (f32[4,128]{1,0:T(4,128)S(1)}, f32[4,128]{1,0:T(4,128)}, u32[]{:S(2)}) copy-start(f32[4,128]{1,0:T(4,128)} %copy-done.206) | copy-start | bytes 6148
  594.3 29.7 %copy-start.265 = (f32[32]{0:T(128)S(1)}, f32[32]{0:T(128)}, u32[]{:S(2)}) copy-start(f32[32]{0:T(128)} %copy-done.264) | copy-start | bytes 388
  596.8 36.0 %copy-start.31 = (f32[128,1024]{1,0:T(8,128)S(1)}, f32[128,1024]{1,0:T(8,128)}, u32[]{:S(2)}) copy-start(f32[128,1024]{1,0:T(8,128)} %copy-done.30) | copy-start | bytes 1572868
  600.2 70.0 %reduce-scatter.45.cloned.1.call-start = ((), (), s32[]{:S(2)}) async-start(), calls=%async_computation.36 | async-start | bytes 655360 | tf_op jit(solution)/shard_map/reduce_scatter | solution.py:78
  640.5 29.7 %copy-start.54 = (f32[32,1024]{1,0:T(8,128)S(1)}, f32[32,1024]{1,0:T(8,128)}, u32[]{:S(2)}) copy-start(f32[32,1024]{1,0:T(8,128)} %copy-done.53) | copy-start | bytes 393220
  640.5 29.7 %copy-start.186 = (f32[1,1024]{1,0:T(1,128)S(1)}, f32[1,1024]{1,0:T(1,128)}, u32[]{:S(2)}) copy-start(f32[1,1024]{1,0:T(1,128)} %copy-done.185) | copy-start | bytes 12292
  640.5 29.7 %copy-start.230 = (f32[32]{0:T(128)S(1)}, f32[32]{0:T(128)}, u32[]{:S(2)}) copy-start(f32[32]{0:T(128)} %copy-done.229) | copy-start | bytes 388
  640.5 29.7 %copy-start.250 = (f32[32]{0:T(128)S(1)}, f32[32]{0:T(128)}, u32[]{:S(2)}) copy-start(f32[32]{0:T(128)} %copy-done.249) | copy-start | bytes 388
  640.5 31.4 %copy-start.263 = (f32[32]{0:T(128)S(1)}, f32[32]{0:T(128)}, u32[]{:S(2)}) copy-start(f32[32]{0:T(128)} %copy-done.262) | copy-start | bytes 388
  640.5 32.5 %copy-start.118 = (f32[32,1024]{1,0:T(8,128)S(1)}, f32[32,1024]{1,0:T(8,128)}, u32[]{:S(2)}) copy-start(f32[32,1024]{1,0:T(8,128)} %copy-done.117) | copy-start | bytes 393220
  648.0 33.4 %copy-start.105 = (f32[4,128,128]{1,2,0:T(8,128)S(1)}, f32[4,128,128]{1,2,0:T(8,128)}, u32[]{:S(2)}) copy-start(f32[4,128,128]{1,2,0:T(8,128)} %copy-done.104) | copy-start | bytes 786436
  648.0 33.4 %copy-start.205 = (f32[4,128]{1,0:T(4,128)S(1)}, f32[4,128]{1,0:T(4,128)}, u32[]{:S(2)}) copy-start(f32[4,128]{1,0:T(4,128)} %copy-done.204) | copy-start | bytes 6148
  648.0 66.4 %reduce-scatter.47.cloned.1.call-start = ((), (), s32[]{:S(2)}) async-start(), calls=%async_computation.37 | async-start | bytes 655360 | tf_op jit(solution)/shard_map/reduce_scatter | solution.py:78
  686.3 29.7 %copy-start.261 = (f32[32]{0:T(128)S(1)}, f32[32]{0:T(128)}, u32[]{:S(2)}) copy-start(f32[32]{0:T(128)} %copy-done.260) | copy-start | bytes 388
  692.1 67.5 %reduce-scatter.49.cloned.1.call-start = ((), (), s32[]{:S(2)}) async-start(), calls=%async_computation.38 | async-start | bytes 655360 | tf_op jit(solution)/shard_map/reduce_scatter | solution.py:78
  737.4 35.2 %copy-start.180 = (f32[1,1024]{1,0:T(1,128)S(1)}, f32[1,1024]{1,0:T(1,128)}, u32[]{:S(2)}) copy-start(f32[1,1024]{1,0:T(1,128)} %copy-done.179) | copy-start | bytes 12292
  737.4 35.3 %copy-start.200 = (f32[4,128]{1,0:T(4,128)S(1)}, f32[4,128]{1,0:T(4,128)}, u32[]{:S(2)}) copy-start(f32[4,128]{1,0:T(4,128)} %copy-done.199) | copy-start | bytes 6148
  737.5 149.8 %reduce-scatter.53.cloned.1.call-start = ((), (), s32[]{:S(2)}) async-start(), calls=%async_computation.40 | async-start | bytes 655360 | tf_op jit(solution)/shard_map/reduce_scatter | solution.py:78
  781.8 108.6 %reduce-scatter.37.cloned.1.call-start = ((), (), s32[]{:S(2)}) async-start(), calls=%async_computation.32 | async-start | bytes 2621440 | tf_op jit(solution)/shard_map/reduce_scatter | solution.py:78
  788.9 101.4 %reduce-scatter.51.cloned.1.call-start = ((), (), s32[]{:S(2)}) async-start(), calls=%async_computation.39 | async-start | bytes 2621440 | tf_op jit(solution)/shard_map/reduce_scatter | solution.py:78
  815.9 1345.8 %all-reduce.4.cloned.1.call-start = ((), (), s32[]{:S(2)}) async-start(), calls=%async_computation.41 | async-start | bytes 80740352 | tf_op jit(solution)/shard_map/psum | solution.py:82
  887.2 54.4 %copy-start.71 = (f32[256,512]{1,0:T(8,128)S(1)}, f32[256,512]{1,0:T(8,128)}, u32[]{:S(2)}) copy-start(f32[256,512]{1,0:T(8,128)} %add_add_fusion.3) | copy-start | bytes 1572868
  890.3 51.3 %copy-start.59 = (f32[256,512]{1,0:T(8,128)S(1)}, f32[256,512]{1,0:T(8,128)}, u32[]{:S(2)}) copy-start(f32[256,512]{1,0:T(8,128)} %reduce-scatter.37.cloned.1.call-done) | copy-start | bytes 1572868
  890.4 51.2 %copy-start.60 = (f32[256,512]{1,0:T(8,128)S(1)}, f32[256,512]{1,0:T(8,128)}, u32[]{:S(2)}) copy-start(f32[256,512]{1,0:T(8,128)} %reduce-scatter.51.cloned.1.call-done) | copy-start | bytes 1572868
  (247 other events, 1711.8 us)
Sparse Core Ops, SparseCore 0:
  13.0 26.4 all-gather.5
  54.0 22.4 reduce-scatter.18
  95.1 22.0 reduce-scatter.20
  133.3 21.9 reduce-scatter.22
  175.4 22.0 reduce-scatter.24
  213.6 22.0 reduce-scatter.26
  237.9 22.5 all-gather.7
  263.7 21.6 reduce-scatter.28
  304.7 31.7 reduce-scatter.30
  338.0 22.5 all-gather.11
  362.8 22.5 all-gather.9
  401.3 31.4 reduce-scatter.34
  435.9 31.3 reduce-scatter.32
  470.6 22.5 all-gather.13
  508.6 21.6 reduce-scatter.38
  556.2 22.0 reduce-scatter.40
  600.3 22.0 reduce-scatter.42
  648.1 22.0 reduce-scatter.44
  692.3 22.0 reduce-scatter.46
  737.6 22.0 reduce-scatter.48
  781.9 22.0 reduce-scatter.52
  806.5 31.4 reduce-scatter.36
  841.2 31.3 reduce-scatter.50
  886.7 1274.9 all-reduce.3
where the time goes:
time: 2220 us; the launch traced here: 2200 us
  waiting for transfers between devices  1610 us (73%)
  matrix products  284 us (13%)
  blocking collectives  142 us (6%)
  local copies, waits for them, and re-layouts  76.6 us (3%)
  other arithmetic  69.8 us (3%)
    psum x1, waiting for transfers between devices, reduce_branch(): return lax.psum(weight_grads, 'dp')  1220 us
    dot_general x56, matrix products, product(): return jnp.dot(left_side, right_side, precision=PRECISE)  186 us
    reduce_scatter x8, waiting for transfers between devices, branch_sum(): lax.psum_scatter(product(source, weight), 'mp', scatter_dimension=0, tile...  169 us
    reduce_scatter x10, waiting for transfers between devices, collect_grads(): return lax.psum_scatter(pieces_in, 'mp', scatter_dimension=0, tiled=True)  152 us
    all_gather x7, blocking collectives, gather_rows(): return lax.all_gather(pieces_in, 'mp', axis=0, tiled=True)  51.9 us
    psum x1, blocking collectives, body(): lax.psum((gains_read[0], gains_read[1], gain_read_mlp, jnp.stack(gains_at...  47.7 us
  transfers between devices with their start and end apart: 24, of which 20 were waited for; matrix products, arithmetic and copies ran while one was open for 8% of the time, Pallas kernels for 0%

commit v1 on v0

--- a/solution.py
+++ b/solution.py
@@ -339,17 +339,20 @@
     grad_x = grad_x + grad_key
     grad_interface = grad_x * keep_rows
     summed_gains = lax.psum(
-        (
-            gains_read[0],
-            gains_read[1],
-            gain_read_mlp,
-            jnp.stack(gains_att_list),
-            jnp.stack(gains_mlp_list),
-            gains_write[0],
-            gains_write[1],
-            gain_write_mlp,
+        lax.psum(
+            (
+                gains_read[0],
+                gains_read[1],
+                gain_read_mlp,
+                jnp.stack(gains_att_list),
+                jnp.stack(gains_mlp_list),
+                gains_write[0],
+                gains_write[1],
+                gain_write_mlp,
+            ),
+            "mp",
         ),
-        ("dp", "mp"),
+        "dp",
     )
     self_qkv_grad = jnp.stack(
         [jnp.stack([entry[0], entry[1], entry[2]]) for entry in grads_att_list]

time: 2220 us -> 2220 us (level)
    psum x0 -> x1, blocking collectives: none -> 41.3 us  [body(): lax.psum(lax.psum((gains_read[0], gains_read[1], gain_read_mlp, jnp.stack...]
    psum x1, blocking collectives: 47.7 us -> 12 us  [body(): lax.psum((gains_read[0], gains_read[1], gain_read_mlp, jnp.stack(gains_at...]
where the time goes in v1:
time: 2220 us; the launch traced here: 2200 us
  waiting for transfers between devices  1610 us (73%)
  matrix products  284 us (13%)
  blocking collectives  148 us (7%)
  local copies, waits for them, and re-layouts  76.5 us (3%)
  other arithmetic  69.7 us (3%)
    psum x1, waiting for transfers between devices, reduce_branch(): return lax.psum(weight_grads, 'dp')  1210 us
    dot_general x56, matrix products, product(): return jnp.dot(left_side, right_side, precision=PRECISE)  186 us
    reduce_scatter x8, waiting for transfers between devices, branch_sum(): lax.psum_scatter(product(source, weight), 'mp', scatter_dimension=0, tile...  170 us
    reduce_scatter x10, waiting for transfers between devices, collect_grads(): return lax.psum_scatter(pieces_in, 'mp', scatter_dimension=0, tiled=True)  152 us
    all_gather x7, blocking collectives, gather_rows(): return lax.all_gather(pieces_in, 'mp', axis=0, tiled=True)  51.8 us
  transfers between devices with their start and end apart: 24, of which 20 were waited for; matrix products, arithmetic and copies ran while one was open for 8% of the time, Pallas kernels for 0%

profile of v1, /device:TPU:0, one launch (start us, length us, event | category | flops | bytes accessed | tf_op | source)
XLA Modules:
  0.0 2203.9 jit_solution(16757406105640829327)
XLA Ops:
  18.9 9.9 all_gather.65
  30.7 8.8 all-gather.6.cloned.1.call-done
  53.8 22.6 %reduce-scatter.19.cloned.1.call-done = f32[32,1024]{1,0:T(8,128)} async-done(((f32[128,1024]{1,0:T(8,128)}), f32[32,1024]{1,0:T(8,128)}) %reduce-scatter.19.cloned.1.call-update) | async-done | bytes 131088 | tf_op jit(solution)/shard_map/reduce_scatter | solution.py:70
  78.7 7.1 all_gather.66
  94.9 5.5 slice_bitcast_fusion
  108.1 8.9 reduce-scatter.21.cloned.1.call-done
  119.1 6.9 all_gather.67
  133.8 21.3 reduce-scatter.23.cloned.1.call-done
  157.1 7.0 all_gather.68
  182.8 14.5 reduce-scatter.25.cloned.1.call-done
  199.5 6.9 all_gather.69
  214.2 21.4 reduce-scatter.27.cloned.1.call-done
  237.5 7.2 all_gather.70
  250.6 5.5 fusion.2
  267.2 18.1 reduce-scatter.29.cloned.1.call-done
  287.4 6.8 all_gather.71
  305.2 31.3 %reduce-scatter.31.cloned.1.call-done = f32[256,512]{1,0:T(8,128)} async-done(((f32[1024,512]{1,0:T(8,128)}), f32[256,512]{1,0:T(8,128)}) %reduce-scatter.31.cloned.1.call-update) | async-done | bytes 524304 | tf_op jit(solution)/shard_map/reduce_scatter | solution.py:70
  340.5 20.1 all-gather.12.cloned.1.call-done
  360.6 6.6 fusion.207
  367.2 18.2 all-gather.10.cloned.1.call-done
  385.4 9.6 fusion.29
  402.3 6.9 fusion.54
  409.3 23.4 %reduce-scatter.35.cloned.1.call-done = f32[256,512]{1,0:T(8,128)} async-done(((f32[1024,512]{1,0:T(8,128)}), f32[256,512]{1,0:T(8,128)}) %reduce-scatter.35.cloned.1.call-update) | async-done | bytes 524304 | tf_op jit(solution)/shard_map/reduce_scatter | solution.py:78
  435.8 31.4 %reduce-scatter.33.cloned.1.call-done = f32[256,512]{1,0:T(8,128)} async-done(((f32[1024,512]{1,0:T(8,128)}), f32[256,512]{1,0:T(8,128)}) %reduce-scatter.33.cloned.1.call-update) | async-done | bytes 524304 | tf_op jit(solution)/shard_map/reduce_scatter | solution.py:70
  470.5 22.7 %all-gather.14.cloned.1.call-done = f32[1024,512]{1,0:T(8,128)} async-done(((f32[256,512]{1,0:T(8,128)}), f32[1024,512]{1,0:T(8,128)}) %all-gather.14.cloned.1.call-update) | async-done | bytes 2097168 | tf_op jit(solution)/shard_map/all_gather | solution.py:74
  508.5 21.8 reduce-scatter.39.cloned.1.call-done
  533.8 7.2 all_gather.76
  541.0 6.9 fusion.75
  548.6 7.3 fusion.4
  559.3 18.9 reduce-scatter.41.cloned.1.call-done
  581.2 7.1 all_gather.77
  600.2 22.2 %reduce-scatter.43.cloned.1.call-done = f32[32,1024]{1,0:T(8,128)} async-done(((f32[128,1024]{1,0:T(8,128)}), f32[32,1024]{1,0:T(8,128)}) %reduce-scatter.43.cloned.1.call-update) | async-done | bytes 131088 | tf_op jit(solution)/shard_map/reduce_scatter | solution.py:78
  625.8 7.0 all_gather.78
  632.8 6.9 fusion.69
  640.5 7.4 fusion.12
  648.0 22.1 %reduce-scatter.45.cloned.1.call-done = f32[32,1024]{1,0:T(8,128)} async-done(((f32[128,1024]{1,0:T(8,128)}), f32[32,1024]{1,0:T(8,128)}) %reduce-scatter.45.cloned.1.call-update) | async-done | bytes 131088 | tf_op jit(solution)/shard_map/reduce_scatter | solution.py:78
  673.1 7.1 all_gather.79
  692.1 22.2 %reduce-scatter.47.cloned.1.call-done = f32[32,1024]{1,0:T(8,128)} async-done(((f32[128,1024]{1,0:T(8,128)}), f32[32,1024]{1,0:T(8,128)}) %reduce-scatter.47.cloned.1.call-update) | async-done | bytes 131088 | tf_op jit(solution)/shard_map/reduce_scatter | solution.py:78
  717.1 7.2 all_gather.80
  724.4 6.8 fusion.213
  738.1 21.5 reduce-scatter.49.cloned.1.call-done
  763.2 6.9 all_gather.81
  789.0 6.9 fusion.222
  868.2 5.5 fusion.178
  893.7 12.0 all-reduce.2
  905.7 41.3 %all-reduce = (f32[1024]{0:T(1024)}, f32[512]{0:T(512)}, f32[1024]{0:T(1024)}, f32[2,1024]{1,0:T(2,128)}, f32[2,1024]{1,0:T(2,128)}, /*index=5*/f32[512]{0:T(512)}, f32[1024]{0:T(1024)}, f32[512]{0:T(512)}) all-reduce(f32[1024]{0:T(1024)S(1)} %get-tuple-element.82, ...), channel_id=1, replica_groups=mesh['dp'=8,'mp'=4] {'dp'}, use_global_device_ids=true, to_apply=%region_70.71 | all-reduce | flops 8704 | bytes 69632 | tf_op jit(solution)/shard_map/psum | solution.py:341
  948.1 1213.6 %all-reduce.5.cloned.1.call-done = (f32[1024,256]{1,0:T(8,128)}, f32[1,512,256]{2,1,0:T(8,128)}, f32[1,512,256]{2,1,0:T(8,128)}, f32[256,1024]{1,0:T(8,128)}, f3...) async-done(((f32[1024,256]{1,0:T(8,128)}, ...) | async-done | bytes 40370192 | tf_op jit(solution)/shard_map/psum | solution.py:82
  2177.8 6.8 pad_maximum_fusion
  (815 shorter events, 344.7 us)
Async XLA Ops:
  7.2 378.2 %copy-start = (f32[512,512]{1,0:T(8,128)S(1)}, f32[512,512]{1,0:T(8,128)}, u32[]{:S(2)}) copy-start(f32[512,512]{1,0:T(8,128)} %param.50) | copy-start | bytes 3145732
  7.2 32.2 %all-gather.6.cloned.1.call-start = ((), (), s32[]{:S(2)}) async-start(), calls=%async_computation.18 | async-start | bytes 2621440 | tf_op jit(solution)/shard_map/all_gather | solution.py:66
  12.9 63.5 %reduce-scatter.19.cloned.1.call-start = ((), (), s32[]{:S(2)}) async-start(), calls=%async_computation.19 | async-start | bytes 655360 | tf_op jit(solution)/shard_map/reduce_scatter | solution.py:70
  53.8 63.2 %reduce-scatter.21.cloned.1.call-start = ((), (), s32[]{:S(2)}) async-start(), calls=%async_computation.20 | async-start | bytes 655360 | tf_op jit(solution)/shard_map/reduce_scatter | solution.py:70
  94.8 60.3 %reduce-scatter.23.cloned.1.call-start = ((), (), s32[]{:S(2)}) async-start(), calls=%async_computation.21 | async-start | bytes 655360 | tf_op jit(solution)/shard_map/reduce_scatter | solution.py:70
  108.0 91.3 %copy-start.183 = (f32[1,1024]{1,0:T(1,128)}, f32[1,1024]{1,0:T(1,128)S(1)}, u32[]{:S(2)}) copy-start(f32[1,1024]{1,0:T(1,128)S(1)} %get-tuple-element.139) | copy-start | bytes 12292
  132.9 64.4 %reduce-scatter.25.cloned.1.call-start = ((), (), s32[]{:S(2)}) async-start(), calls=%async_computation.22 | async-start | bytes 655360 | tf_op jit(solution)/shard_map/reduce_scatter | solution.py:70
  133.8 35.0 %copy-start.185 = (f32[1,1024]{1,0:T(1,128)}, f32[1,1024]{1,0:T(1,128)S(1)}, u32[]{:S(2)}) copy-start(f32[1,1024]{1,0:T(1,128)S(1)} %get-tuple-element.138) | copy-start | bytes 12292
  133.8 103.6 %copy-start.187 = (f32[1,1024]{1,0:T(1,128)}, f32[1,1024]{1,0:T(1,128)S(1)}, u32[]{:S(2)}) copy-start(f32[1,1024]{1,0:T(1,128)S(1)} %get-tuple-element.137) | copy-start | bytes 12292
  175.1 60.4 %reduce-scatter.27.cloned.1.call-start = ((), (), s32[]{:S(2)}) async-start(), calls=%async_computation.23 | async-start | bytes 655360 | tf_op jit(solution)/shard_map/reduce_scatter | solution.py:70
  213.4 49.2 %all-gather.8.cloned.1.call-start = ((), (), s32[]{:S(2)}) async-start(), calls=%async_computation.25 | async-start | bytes 2621440 | tf_op jit(solution)/shard_map/all_gather | solution.py:66
  214.1 71.2 %reduce-scatter.29.cloned.1.call-start = ((), (), s32[]{:S(2)}) async-start(), calls=%async_computation.24 | async-start | bytes 655360 | tf_op jit(solution)/shard_map/reduce_scatter | solution.py:70
  256.2 80.3 %reduce-scatter.31.cloned.1.call-start = ((), (), s32[]{:S(2)}) async-start(), calls=%async_computation.26 | async-start | bytes 2621440 | tf_op jit(solution)/shard_map/reduce_scatter | solution.py:70
  304.5 56.0 %all-gather.12.cloned.1.call-start = ((), (), s32[]{:S(2)}) async-start(), calls=%async_computation.29 | async-start | bytes 2621440 | tf_op jit(solution)/shard_map/all_gather | solution.py:74
  305.1 80.3 %all-gather.10.cloned.1.call-start = ((), (), s32[]{:S(2)}) async-start(), calls=%async_computation.27 | async-start | bytes 2621440 | tf_op jit(solution)/shard_map/all_gather | solution.py:66
  340.2 92.5 %reduce-scatter.35.cloned.1.call-start = ((), (), s32[]{:S(2)}) async-start(), calls=%async_computation.30 | async-start | bytes 2621440 | tf_op jit(solution)/shard_map/reduce_scatter | solution.py:78
  401.1 66.1 %reduce-scatter.33.cloned.1.call-start = ((), (), s32[]{:S(2)}) async-start(), calls=%async_computation.28 | async-start | bytes 2621440 | tf_op jit(solution)/shard_map/reduce_scatter | solution.py:70
  409.3 60.2 %copy-start.111 = (f32[256,512]{1,0:T(8,128)S(1)}, f32[256,512]{1,0:T(8,128)}, u32[]{:S(2)}) copy-start(f32[256,512]{1,0:T(8,128)} %param.52) | copy-start | bytes 1572868
  409.3 83.9 %all-gather.14.cloned.1.call-start = ((), (), s32[]{:S(2)}) async-start(), calls=%async_computation.31 | async-start | bytes 2621440 | tf_op jit(solution)/shard_map/all_gather | solution.py:74
  470.4 59.8 %reduce-scatter.39.cloned.1.call-start = ((), (), s32[]{:S(2)}) async-start(), calls=%async_computation.33 | async-start | bytes 655360 | tf_op jit(solution)/shard_map/reduce_scatter | solution.py:78
  507.0 34.0 %copy-start.34 = (f32[128,1024]{1,0:T(8,128)S(1)}, f32[128,1024]{1,0:T(8,128)}, u32[]{:S(2)}) copy-start(f32[128,1024]{1,0:T(8,128)} %copy-done.33) | copy-start | bytes 1572868
  508.5 69.7 %reduce-scatter.41.cloned.1.call-start = ((), (), s32[]{:S(2)}) async-start(), calls=%async_computation.34 | async-start | bytes 655360 | tf_op jit(solution)/shard_map/reduce_scatter | solution.py:78
  556.1 66.2 %reduce-scatter.43.cloned.1.call-start = ((), (), s32[]{:S(2)}) async-start(), calls=%async_computation.35 | async-start | bytes 655360 | tf_op jit(solution)/shard_map/reduce_scatter | solution.py:78
  559.3 30.0 %copy-start.107 = (f32[4,128,128]{1,2,0:T(8,128)S(1)}, f32[4,128,128]{1,2,0:T(8,128)}, u32[]{:S(2)}) copy-start(f32[4,128,128]{1,2,0:T(8,128)} %copy-done.106) | copy-start | bytes 786436
  559.3 30.0 %copy-start.207 = (f32[4,128]{1,0:T(4,128)S(1)}, f32[4,128]{1,0:T(4,128)}, u32[]{:S(2)}) copy-start(f32[4,128]{1,0:T(4,128)} %copy-done.206) | copy-start | bytes 6148
  594.2 29.7 %copy-start.265 = (f32[32]{0:T(128)S(1)}, f32[32]{0:T(128)}, u32[]{:S(2)}) copy-start(f32[32]{0:T(128)} %copy-done.264) | copy-start | bytes 388
  596.8 36.0 %copy-start.31 = (f32[128,1024]{1,0:T(8,128)S(1)}, f32[128,1024]{1,0:T(8,128)}, u32[]{:S(2)}) copy-start(f32[128,1024]{1,0:T(8,128)} %copy-done.30) | copy-start | bytes 1572868
  600.1 70.0 %reduce-scatter.45.cloned.1.call-start = ((), (), s32[]{:S(2)}) async-start(), calls=%async_computation.36 | async-start | bytes 655360 | tf_op jit(solution)/shard_map/reduce_scatter | solution.py:78
  640.5 29.7 %copy-start.54 = (f32[32,1024]{1,0:T(8,128)S(1)}, f32[32,1024]{1,0:T(8,128)}, u32[]{:S(2)}) copy-start(f32[32,1024]{1,0:T(8,128)} %copy-done.53) | copy-start | bytes 393220
  640.5 29.7 %copy-start.186 = (f32[1,1024]{1,0:T(1,128)S(1)}, f32[1,1024]{1,0:T(1,128)}, u32[]{:S(2)}) copy-start(f32[1,1024]{1,0:T(1,128)} %copy-done.185) | copy-start | bytes 12292
  640.5 29.7 %copy-start.230 = (f32[32]{0:T(128)S(1)}, f32[32]{0:T(128)}, u32[]{:S(2)}) copy-start(f32[32]{0:T(128)} %copy-done.229) | copy-start | bytes 388
  640.5 29.7 %copy-start.250 = (f32[32]{0:T(128)S(1)}, f32[32]{0:T(128)}, u32[]{:S(2)}) copy-start(f32[32]{0:T(128)} %copy-done.249) | copy-start | bytes 388
  640.5 31.4 %copy-start.263 = (f32[32]{0:T(128)S(1)}, f32[32]{0:T(128)}, u32[]{:S(2)}) copy-start(f32[32]{0:T(128)} %copy-done.262) | copy-start | bytes 388
  640.5 32.5 %copy-start.118 = (f32[32,1024]{1,0:T(8,128)S(1)}, f32[32,1024]{1,0:T(8,128)}, u32[]{:S(2)}) copy-start(f32[32,1024]{1,0:T(8,128)} %copy-done.117) | copy-start | bytes 393220
  647.9 33.4 %copy-start.105 = (f32[4,128,128]{1,2,0:T(8,128)S(1)}, f32[4,128,128]{1,2,0:T(8,128)}, u32[]{:S(2)}) copy-start(f32[4,128,128]{1,2,0:T(8,128)} %copy-done.104) | copy-start | bytes 786436
  647.9 33.4 %copy-start.205 = (f32[4,128]{1,0:T(4,128)S(1)}, f32[4,128]{1,0:T(4,128)}, u32[]{:S(2)}) copy-start(f32[4,128]{1,0:T(4,128)} %copy-done.204) | copy-start | bytes 6148
  648.0 66.3 %reduce-scatter.47.cloned.1.call-start = ((), (), s32[]{:S(2)}) async-start(), calls=%async_computation.37 | async-start | bytes 655360 | tf_op jit(solution)/shard_map/reduce_scatter | solution.py:78
  686.2 29.7 %copy-start.261 = (f32[32]{0:T(128)S(1)}, f32[32]{0:T(128)}, u32[]{:S(2)}) copy-start(f32[32]{0:T(128)} %copy-done.260) | copy-start | bytes 388
  692.1 67.5 %reduce-scatter.49.cloned.1.call-start = ((), (), s32[]{:S(2)}) async-start(), calls=%async_computation.38 | async-start | bytes 655360 | tf_op jit(solution)/shard_map/reduce_scatter | solution.py:78
  737.4 35.2 %copy-start.180 = (f32[1,1024]{1,0:T(1,128)S(1)}, f32[1,1024]{1,0:T(1,128)}, u32[]{:S(2)}) copy-start(f32[1,1024]{1,0:T(1,128)} %copy-done.179) | copy-start | bytes 12292
  737.4 35.2 %copy-start.200 = (f32[4,128]{1,0:T(4,128)S(1)}, f32[4,128]{1,0:T(4,128)}, u32[]{:S(2)}) copy-start(f32[4,128]{1,0:T(4,128)} %copy-done.199) | copy-start | bytes 6148
  737.4 149.6 %reduce-scatter.53.cloned.1.call-start = ((), (), s32[]{:S(2)}) async-start(), calls=%async_computation.40 | async-start | bytes 655360 | tf_op jit(solution)/shard_map/reduce_scatter | solution.py:78
  781.6 108.5 %reduce-scatter.37.cloned.1.call-start = ((), (), s32[]{:S(2)}) async-start(), calls=%async_computation.32 | async-start | bytes 2621440 | tf_op jit(solution)/shard_map/reduce_scatter | solution.py:78
  788.8 101.3 %reduce-scatter.51.cloned.1.call-start = ((), (), s32[]{:S(2)}) async-start(), calls=%async_computation.39 | async-start | bytes 2621440 | tf_op jit(solution)/shard_map/reduce_scatter | solution.py:78
  815.7 1346.1 %all-reduce.5.cloned.1.call-start = ((), (), s32[]{:S(2)}) async-start(), calls=%async_computation.41 | async-start | bytes 80740352 | tf_op jit(solution)/shard_map/psum | solution.py:82
  888.1 58.8 %copy-start.71 = (f32[256,512]{1,0:T(8,128)S(1)}, f32[256,512]{1,0:T(8,128)}, u32[]{:S(2)}) copy-start(f32[256,512]{1,0:T(8,128)} %add_add_fusion.3) | copy-start | bytes 1572868
  890.1 56.9 %copy-start.59 = (f32[256,512]{1,0:T(8,128)S(1)}, f32[256,512]{1,0:T(8,128)}, u32[]{:S(2)}) copy-start(f32[256,512]{1,0:T(8,128)} %reduce-scatter.37.cloned.1.call-done) | copy-start | bytes 1572868
  890.1 56.8 %copy-start.60 = (f32[256,512]{1,0:T(8,128)S(1)}, f32[256,512]{1,0:T(8,128)}, u32[]{:S(2)}) copy-start(f32[256,512]{1,0:T(8,128)} %reduce-scatter.51.cloned.1.call-done) | copy-start | bytes 1572868
  (247 other events, 1711.1 us)
Sparse Core Ops, SparseCore 0:
  13.0 26.4 all-gather.5
  53.9 22.4 reduce-scatter.18
  94.9 22.0 reduce-scatter.20
  133.1 22.0 reduce-scatter.22
  175.3 22.0 reduce-scatter.24
  213.5 22.0 reduce-scatter.26
  237.8 22.5 all-gather.7
  263.6 21.6 reduce-scatter.28
  304.7 31.7 reduce-scatter.30
  338.0 22.5 all-gather.11
  362.8 22.5 all-gather.9
  401.3 31.4 reduce-scatter.34
  435.8 31.3 reduce-scatter.32
  470.5 22.5 all-gather.13
  508.6 21.6 reduce-scatter.38
  556.1 22.0 reduce-scatter.40
  600.2 22.0 reduce-scatter.42
  648.1 22.0 reduce-scatter.44
  692.2 22.0 reduce-scatter.46
  737.5 22.0 reduce-scatter.48
  781.7 22.0 reduce-scatter.52
  806.3 31.4 reduce-scatter.36
  841.1 31.3 reduce-scatter.50
  886.4 1275.2 all-reduce.4
